TPU v7x, 32 devices: a whole 2x2x4 slice. The times are simulated.
32 devices in a mesh: row: 4 (over y, core), col: 8 (over z, x).
Axes of the slice: x: 2, y: 2, z: 4, core: 2. Of those that a mesh axis runs over, the one named last changes fastest.
Arguments:
- normal: float32 [16, 4, 256, 8, 8, 256], P(None, 'row', None, None, 'col'), may hold values from -1.5 to 1.5
- panel_inverse: float32 [256, 256], replicated, as said below
- rhs: float32 [16, 4, 256, 512], P(None, 'row', None, 'col'), may hold values from -0.009765625 to 0.009765625
- shifts: float32 [4], replicated, may hold values from 16 to 128
Outputs:
- schur: float32 [16, 4, 256, 8, 8, 256], P(None, 'row', None, None, 'col')
- eliminated: float32 [16, 4, 256, 512], P(None, 'row', None, 'col')
- applied: float32 [16, 4, 256, 512], P(None, 'row', None, 'col')
Inputs may be any that keep to these rules, and one draw needn't show every extreme that they name: `panel_inverse`: lower triangular with positive diagonal entries.
All inputs are finite; a program needn't handle non-finite values.
Results may differ from a plain program's by a relative error of at most 0.000076.
Values sent between devices are 32-bit elements; how exact they have to be, the bound alone decides.
A program may use at most 256 MiB of HBM per device.

v0:
```python
import jax
import jax.numpy as jnp
from jax import lax
from jax.sharding import PartitionSpec as P

R = 128


def spread_2(value, axis, source):
    kept = jnp.where(lax.axis_index(axis) == source, value, 0).astype(value.dtype)
    return lax.psum(kept, axis)


def pick_blocks(blocks, spacing, offset):
    grouped = blocks.reshape((blocks.shape[0] // spacing, spacing) + blocks.shape[1:])
    return lax.dynamic_index_in_dim(grouped, offset, 1, keepdims=False)


def shards(normal, panel_inverse, rhs, shifts):
    high = lax.Precision.HIGHEST
    row_index = lax.axis_index("row")
    col_index = lax.axis_index("col")
    nrow = lax.axis_size("row")
    ncol = lax.axis_size("col")
    spacing = ncol // nrow
    brows, nb, bcols = (normal.shape[0], normal.shape[2], normal.shape[3])
    narrow = rhs.shape[3]
    wide = narrow * ncol
    tile = normal.reshape(brows * nb, bcols * nb)
    owner = col_index % nrow
    offset = col_index // nrow
    local_panel = jnp.dot(
        tile[:, :nb], panel_inverse.T, precision=high, preferred_element_type=jnp.float32
    )
    panel = spread_2(local_panel, "col", 0)
    chosen = pick_blocks(panel.reshape(brows, nb, nb), spacing, offset)
    crossed = spread_2(chosen, "row", owner).reshape(bcols * nb, nb)
    updated = tile - jnp.dot(panel, crossed.T, precision=high, preferred_element_type=jnp.float32)
    leading = spread_2(rhs[0, 0], "row", 0)
    first = jnp.dot(panel_inverse, leading, precision=high, preferred_element_type=jnp.float32)
    reduced = rhs.reshape(brows * nb, narrow) - jnp.dot(
        panel, first, precision=high, preferred_element_type=jnp.float32
    )
    reduced = reduced.reshape(brows, nb, narrow)
    reduced = reduced.at[0].set(jnp.where(row_index == 0, first, reduced[0]))
    spread = lax.all_gather(reduced, "col", axis=2, tiled=True)
    scales = lax.dynamic_slice_in_dim(jnp.repeat(shifts, R), col_index * narrow, narrow)
    partial_value = lax.dot_general(
        updated,
        spread.reshape(brows * nb, wide),
        (((0,), (0,)), ((), ())),
        precision=high,
        preferred_element_type=jnp.float32,
    )
    totals = lax.psum(partial_value, "row")
    totals = totals.reshape(bcols, nb, ncol, narrow)
    arrived = lax.all_to_all(totals, "col", split_axis=2, concat_axis=2, tiled=True)
    arrived = arrived.reshape(bcols, nb, spacing, nrow, narrow)
    arrived = lax.dynamic_index_in_dim(arrived, row_index, 3, keepdims=False)
    product = jnp.transpose(arrived, (0, 2, 1, 3)).reshape(brows, nb, narrow)
    applied = product + reduced * scales[None, None, :]
    schur = updated.reshape(brows, 1, nb, bcols, 1, nb)
    return (schur, reduced.reshape(brows, 1, nb, narrow), applied.reshape(brows, 1, nb, narrow))


def solution(mesh):
    in_specs = (P(None, "row", None, None, "col", None), P(), P(None, "row", None, "col"), P())
    out_specs = (
        P(None, "row", None, None, "col", None),
        P(None, "row", None, "col"),
        P(None, "row", None, "col"),
    )
    return jax.shard_map(shards, mesh=mesh, in_specs=in_specs, out_specs=out_specs, check_vma=False)
```

profile of v0, /device:TPU:0, one launch (start us, length us, event | category | flops | bytes accessed | tf_op | source)
XLA Modules:
  0.0 759.2 jit_solution(6350466244515718778)
XLA Ops:
  7.2 93.9 %reduce.2 = f32[16,256,8,256]{3,2,1,0:T(8,128)} reduce(f32[16,1,256,8,1,256]{5,4,3,2,1,0:T(1,128)} %param.6, f32[]{:T(128)} %constant.77), dimensions={1,4}, to_apply=%param.6.reduce_sub_computation | reduce | bytes 67108864 | tf_op args[0]
  101.1 29.9 %copy.37 = f32[512,8,8,256]{3,1,2,0:T(8,128)} copy(f32[512,8,8,256]{3,2,1,0:T(8,128)} %bitcast.49) | data formatting | bytes 67108864
  131.1 7.7 %convolution_select_fusion = f32[4096,256]{1,0:T(8,128)} fusion(f32[256,256]{1,0:T(8,128)S(1)} %copy-done, f32[4096,2048]{1,0:T(8,128)} %bitcast.47, pred[]{:T(512)S(6)} %eq.12), kind=kOutput, calls=%fused_computation.1 | convolution fusion | flops 3222274048 | bytes 8650753 | tf_op jit(solution)/shard_map/dot_general | solution.py:32
  138.8 1.1 copy-done.5
  139.9 0.6 select_bitcast_fusion
  140.6 157.4 %all-reduce.5.cloned.1.call-done = f32[4096,256]{1,0:T(8,128)} async-done(((f32[4096,256]{1,0:T(8,128)}), f32[4096,256]{1,0:T(8,128)}) %all-reduce.5.cloned.1.call-update) | async-done | bytes 4194320 | tf_op jit(solution)/shard_map/psum | solution.py:11
  298.0 3.1 dynamic-slice_select_fusion
  301.1 0.2 all-gather.2.cloned.1.call-start
  301.3 0.1 copy.38
  301.4 51.3 %all-reduce.9.cloned.1.call-done = (f32[2048,256]{1,0:T(8,128)}, f32[256,64]{0,1:T(8,128)}) async-done(((f32[2048,256]{1,0:T(8,128)}, f32[256,64]{0,1:T(8,128)}), (f32[2048,256]{1,0:T(8,128)}, f32[256,64]{0,1:T(8,128)})) %all-reduce.9.cloned.1.call-update) | async-done | bytes 2162704 | tf_op jit(solution)/shard_map/psum | solution.py:11
  352.7 1.2 fusion.3
  354.0 6.5 convolution_subtract_fusion.1
  360.5 0.1 copy.27
  360.6 0.3 copy.39
  360.9 0.9 scatter.4
  361.8 1.0 copy-done.2
  362.9 34.1 %convolution_subtract_fusion = f32[4096,2048]{1,0:T(8,128)} fusion(f32[4096,2048]{1,0:T(8,128)} %bitcast.48, f32[4096,256]{1,0:T(8,128)} %all-reduce.5.cloned.1.call-done, f32[2048,256]{1,0:T(8,128)S(1)} %copy-done.4), kind=kOutput, calls=%fused_computation | convolution fusion | flops 25778192384 | bytes 73400320 | tf_op jit(solution)/shard_map/dot_general | solution.py:38
  397.0 90.5 %all-gather.2.cloned.1.call-done = f32[16,256,512]{1,0,2:T(8,128)} async-done(((f32[16,256,64]{1,0,2:T(8,128)}), f32[16,256,512]{1,0,2:T(8,128)}) %all-gather.2.cloned.1.call-update) | async-done | bytes 8388624 | tf_op jit(solution)/shard_map/all_gather | solution.py:46
  487.5 9.9 %copy.28 = f32[16,256,512]{2,1,0:T(8,128)} copy(f32[16,256,512]{1,0,2:T(8,128)} %all-gather.2.cloned.1.call-done) | data formatting | bytes 16777216 | tf_op jit(solution)/shard_map/all_gather | solution.py:46
  497.4 64.6 %fusion.4 = f32[2048,512]{0,1:T(8,128)S(1)} fusion(f32[4096,2048]{1,0:T(8,128)} %convolution_subtract_fusion, f32[4096,512]{1,0:T(8,128)} %bitcast.55), kind=kOutput, calls=%fused_computation.13 | convolution fusion | flops 51539607552 | bytes 46137344 | tf_op jit(solution)/shard_map/dot_general | solution.py:48
  562.0 4.0 copy.40
  566.0 83.8 %all-reduce.7.cloned.1.call-done = f32[8,256,8,64]{1,0,3,2:T(8,128)} async-done(((f32[8,256,8,64]{1,0,3,2:T(8,128)}), f32[8,256,8,64]{1,0,3,2:T(8,128)}) %all-reduce.7.cloned.1.call-update) | async-done | bytes 4194320 | tf_op jit(solution)/shard_map/psum | solution.py:55
  649.8 5.5 all-to-all-start
  655.3 0.1 broadcast_bitcast_fusion
  655.4 0.1 dynamic_slice.13
  655.5 48.4 %reshape.98 = f32[16,1,256,8,1,256]{5,4,3,2,1,0:T(1,128)} reshape(f32[4096,2048]{1,0:T(8,128)} %convolution_subtract_fusion) | data formatting | bytes 67108864 | tf_op jit(solution)/shard_map/reshape | solution.py:62
  703.9 1.6 copy.33
  705.5 42.8 %all-to-all-done = f32[8,256,8,64]{1,0,3,2:T(8,128)} async-done(((f32[8,256,8,64]{1,0,3,2:T(8,128)}), f32[8,256,8,64]{1,0,3,2:T(8,128)}, u32[]{:S(2)}, u32[]{:S(2)}) %all-to-all-start) | async-done | bytes 4194336 | tf_op jit(solution)/shard_map/all_to_all | solution.py:57
  748.3 1.3 constant_dynamic-slice_fusion
  749.6 0.3 copy.36
  750.0 0.7 fusion.1
  750.7 1.6 copy.34
  (20 shorter events, 0.2 us)
Async XLA Ops:
  7.2 123.9 %copy-start = (f32[256,256]{1,0:T(8,128)S(1)}, f32[256,256]{1,0:T(8,128)}, u32[]{:S(2)}) copy-start(f32[256,256]{1,0:T(8,128)} %param.7) | copy-start | bytes 786436
  7.2 290.8 %all-reduce.5.cloned.1.call-start = ((), (), s32[]{:S(2)}) async-start(), calls=%async_computation.1 | async-start | bytes 8388608 | tf_op jit(solution)/shard_map/psum | solution.py:11
  138.7 1.2 copy-start.5
  138.7 214.0 %all-reduce.9.cloned.1.call-start = ((), (), s32[]{:S(2)}) async-start(), calls=%async_computation.4 | async-start | bytes 4325376 | tf_op jit(solution)/shard_map/psum | solution.py:11
  301.1 186.4 %all-gather.2.cloned.1.call-start = ((), (), s32[]{:S(2)}) async-start(), calls=%async_computation.2 | async-start | bytes 9437184 | tf_op jit(solution)/shard_map/all_gather | solution.py:46
  354.0 8.9 %copy-start.4 = (f32[2048,256]{1,0:T(8,128)S(1)}, f32[2048,256]{1,0:T(8,128)}, u32[]{:S(2)}) copy-start(f32[2048,256]{1,0:T(8,128)} %get-tuple-element.27) | copy-start | bytes 6291460
  361.8 1.0 copy-start.2
  362.8 287.0 %all-reduce.7.cloned.1.call-start = ((), (), s32[]{:S(2)}) async-start(), calls=%async_computation.3 | async-start | bytes 8388608 | tf_op jit(solution)/shard_map/psum | solution.py:55
  566.0 89.3 %copy-start.6 = (f32[4]{0:T(128)S(1)}, f32[4]{0:T(128)}, u32[]{:S(2)}) copy-start(f32[4]{0:T(128)} %param.9) | copy-start | bytes 52
  649.8 98.5 %all-to-all-start = ((f32[8,256,8,64]{1,0,3,2:T(8,128)}), f32[8,256,8,64]{1,0,3,2:T(8,128)}, u32[]{:S(2)}, u32[]{:S(2)}) async-start(f32[8,256,8,64]{1,0,3,2:T(8,128)} %all-reduce.7.cloned.1.call-done), calls=%async_computation | async-start | bytes 8388608 | tf_op jit(solution)/shard_map/all_to_all | solution.py:57
  655.5 48.4 %copy-start.3 = (f32[16,256,64]{1,0,2:T(8,128)S(1)}, f32[16,256,64]{1,0,2:T(8,128)}, u32[]{:S(2)}) copy-start(f32[16,256,64]{1,0,2:T(8,128)} %copy-done.2) | copy-start | bytes 3145732
  748.3 3.9 copy-start.1
Sparse Core Ops, SparseCore 0:
  138.9 159.0 all-reduce.4
  301.2 51.4 all-reduce.8
  362.9 124.5 all-gather.1
  566.1 83.6 all-reduce.6
where the time goes:
time: 768 us; the launch traced here: 759 us
  waiting for transfers between devices  426 us (55%)
  matrix products  114 us (15%)
  local copies, waits for them, and re-layouts  101 us (13%)
  other arithmetic  98.3 us (13%)
  between operations  14.4 us (2%)
    psum x2, waiting for transfers between devices, spread_2(): return lax.psum(kept, axis)  209 us
    unnamed x1, other arithmetic  93.9 us
    all_gather x1, waiting for transfers between devices, shards(): spread = lax.all_gather(reduced, 'col', axis=2, tiled=True)  90.5 us
    psum x1, waiting for transfers between devices, shards(): totals = lax.psum(partial_value, 'row')  83.8 us
    dot_general x1, matrix products, shards(): lax.dot_general(updated, spread.reshape(brows * nb, wide), (((0,), (0,)),...  64.6 us
    reshape x1, local copies, waits for them, and re-layouts, shards(): schur = updated.reshape(brows, 1, nb, bcols, 1, nb)  48.4 us
    all_to_all x1, waiting for transfers between devices, shards(): lax.all_to_all(totals, 'col', split_axis=2, concat_axis=2, tiled=True)  42.8 us
    unnamed x21, local copies, waits for them, and re-layouts  39.9 us
  transfers between devices with their start and end apart: 5, of which 5 were waited for; matrix products, arithmetic and copies ran while one was open for 11% of the time, Pallas kernels for 0%

commit v1 on v0

v1 whole, which is shorter than its diff:
```python
import functools

import jax
import jax.numpy as jnp
from jax import lax
from jax.experimental import pallas as pl
from jax.experimental.pallas import tpu as pltpu
from jax.sharding import PartitionSpec as P

R = 128
LANES = 128
F32 = jnp.float32
BF16 = jnp.bfloat16


def split(value):
    high = value.astype(BF16)
    low = (value - high.astype(F32)).astype(BF16)
    return high, low


def left_of(value):
    high, low = split(value)
    return jnp.concatenate([high, high, low], axis=1)


def right_of(value):
    high, low = split(value)
    return jnp.concatenate([high, low, high], axis=0)


def dot(left, right):
    return jnp.dot(left, right, preferred_element_type=F32)


def fused_kernel(bcols, nb, narrow, tile_ref, panel_ref, across_ref, rhs_ref, first_ref,
                 schur_ref, own_ref, total_ref, across3, first3, reduced):
    step = pl.program_id(0)
    stride = bcols * nb // LANES
    per = nb // LANES
    wide = first_ref.shape[0]

    @pl.when(step == 0)
    def _():
        across3[...] = right_of(across_ref[...])
        first3[...] = left_of(first_ref[...])
        total_ref[...] = jnp.zeros_like(total_ref)

    panel = panel_ref[...]
    panel3 = left_of(panel)
    high, low = split(panel)
    flat3 = jnp.concatenate([high, low, high], axis=1)
    lowered = lax.dot_general(
        first3[...], flat3, (((1,), (1,)), ((), ())), preferred_element_type=F32
    )
    value = rhs_ref[...].reshape(wide, nb) - lowered
    leading = jnp.logical_and(step == 0, lax.axis_index("row") == 0)
    value = jnp.where(leading, first_ref[...], value)
    reduced[...] = value
    mine = pl.multiple_of(lax.axis_index("col") * narrow, narrow)
    own_ref[0] = reduced[pl.ds(mine, narrow), :]
    value3 = left_of(value)
    for b in range(bcols):
        columns = slice(b * nb, (b + 1) * nb)
        product = dot(panel3, across3[:, columns])
        parts = []
        for h in range(per):
            rows = pl.ds(b * per + h, nb, stride=stride)
            part = tile_ref[rows, :] - product[:, h * LANES:(h + 1) * LANES]
            schur_ref[rows, :] = part
            parts.append(part)
        updated = jnp.concatenate(parts, axis=1)
        total_ref[:, columns] += dot(value3, right_of(updated))


def fused(tile, panel, across, gathered, first, brows, bcols, nb, narrow):
    wide = first.shape[0]
    ncol = wide // narrow
    chunk = nb * bcols * nb // LANES
    whole = lambda i: (0, 0)
    return pl.pallas_call(
        functools.partial(fused_kernel, bcols, nb, narrow),
        grid=(brows,),
        in_specs=[
            pl.BlockSpec((chunk, LANES), lambda i: (i, 0)),
            pl.BlockSpec((nb, nb), lambda i: (i, 0)),
            pl.BlockSpec((nb, bcols * nb), whole),
            pl.BlockSpec((ncol, None, narrow, nb), lambda i: (0, i, 0, 0)),
            pl.BlockSpec((wide, nb), whole),
        ],
        out_specs=[
            pl.BlockSpec((chunk, LANES), lambda i: (i, 0)),
            pl.BlockSpec((1, narrow, nb), lambda i: (i, 0, 0)),
            pl.BlockSpec((wide, bcols * nb), whole),
        ],
        out_shape=[
            jax.ShapeDtypeStruct(tile.shape, F32),
            jax.ShapeDtypeStruct((brows, narrow, nb), F32),
            jax.ShapeDtypeStruct((wide, bcols * nb), F32),
        ],
        scratch_shapes=[
            pltpu.VMEM((3 * nb, bcols * nb), BF16),
            pltpu.VMEM((wide, 3 * nb), BF16),
            pltpu.VMEM((wide, nb), F32),
        ],
        compiler_params=pltpu.CompilerParams(
            dimension_semantics=("arbitrary",), vmem_limit_bytes=48 * 2**20
        ),
    )(tile, panel, across, gathered, first)


def spread(value, axis, source):
    return lax.psum(jnp.where(lax.axis_index(axis) == source, value, 0.0), axis)


def shards(normal, panel_inverse, rhs, shifts):
    high = lax.Precision.HIGHEST
    row_index = lax.axis_index("row")
    col_index = lax.axis_index("col")
    nrow = lax.axis_size("row")
    ncol = lax.axis_size("col")
    spacing = ncol // nrow
    brows, nb, bcols = (normal.shape[0], normal.shape[2], normal.shape[3])
    narrow = rhs.shape[3]
    wide = narrow * ncol
    right = jnp.transpose(rhs[:, 0], (0, 2, 1))
    across = spread(normal[0, 0].reshape(nb, bcols * nb), "row", 0)
    leading = spread(right[0], "row", 0)
    gathered = lax.all_gather(jnp.concatenate([right, leading[None]], axis=0), "col", axis=0)
    column = spread(normal[:, 0, :, 0, 0, :].reshape(brows * nb, nb), "col", 0)
    panel = jnp.dot(column, panel_inverse.T, precision=high, preferred_element_type=F32)
    across = jnp.dot(panel_inverse, across, precision=high, preferred_element_type=F32)
    first = jnp.dot(
        gathered[:, brows].reshape(wide, nb), panel_inverse.T, precision=high,
        preferred_element_type=F32,
    )
    tile = normal.reshape(brows * nb * bcols * nb // LANES, LANES)
    schur, reduced, total = fused(
        tile, panel, across, gathered, first, brows, bcols, nb, narrow
    )
    part = lax.psum_scatter(total, "row", scatter_dimension=0, tiled=True)
    part = part.reshape(spacing, narrow, bcols * nb)
    offset = col_index // nrow
    arrived = []
    for t in range(spacing):
        moves = [
            (p * ncol + q, (q % nrow) * ncol + spacing * p + (q // nrow + t) % spacing)
            for p in range(nrow)
            for q in range(ncol)
        ]
        piece = lax.dynamic_index_in_dim(part, (offset + t) % spacing, 0, keepdims=False)
        arrived.append(lax.ppermute(piece, ("row", "col"), moves))
    arrived = jnp.stack(arrived)
    place = col_index % spacing
    ordered = [
        lax.dynamic_index_in_dim(arrived, (place - o + spacing) % spacing, 0, keepdims=False)
        for o in range(spacing)
    ]
    product = jnp.stack([o.reshape(narrow, bcols, nb) for o in ordered])
    product = jnp.transpose(product, (2, 0, 1, 3)).reshape(brows, narrow, nb)
    scales = lax.dynamic_slice_in_dim(jnp.repeat(shifts, R), col_index * narrow, narrow)
    applied = product + reduced * scales[None, :, None]
    back = lambda value: jnp.transpose(value, (0, 2, 1)).reshape(brows, 1, nb, narrow)
    return (schur.reshape(normal.shape), back(reduced), back(applied))


def solution(mesh):
    in_specs = (P(None, "row", None, None, "col", None), P(), P(None, "row", None, "col"), P())
    out_specs = (
        P(None, "row", None, None, "col", None),
        P(None, "row", None, "col"),
        P(None, "row", None, "col"),
    )
    return jax.shard_map(shards, mesh=mesh, in_specs=in_specs, out_specs=out_specs, check_vma=False)
```

time: 768 us -> 549 us (0.71); the launches traced: 759 us -> 549 us
  matrix products: 114 us -> 11.8 us
  local copies, waits for them, and re-layouts: 101 us -> 8.08 us
  other arithmetic: 98.3 us -> 17.6 us
  Pallas kernels: 0 us -> 76.3 us
  waiting for transfers between devices: 426 us -> 417 us
    dot_general x5 -> x3, matrix products: 114 us -> 11.8 us  [the longest x1 7.58 us: shards(): jnp.dot(column, panel_inverse.T, precision=high, preferred_element_type=F32)]
    unnamed x1 -> x0, other arithmetic: 93.9 us -> none
    psum x3 -> x2, waiting for transfers between devices: 293 us -> 202 us  [spread(): return lax.psum(jnp.where(lax.axis_index(axis) == source, value, 0.0), axis)]
    pallas_call x0 -> x1, Pallas kernels: none -> 76.3 us  [fused(): pl.pallas_call(functools.partial(fused_kernel, bcols, nb, narrow), grid=(...]
    reshape x1 -> x0, local copies, waits for them, and re-layouts: 48.4 us -> none  [shards(): schur = updated.reshape(brows, 1, nb, bcols, 1, nb)]
    ppermute x0 -> x2, waiting for transfers between devices: none -> 48.1 us  [shards(): arrived.append(lax.ppermute(piece, ('row', 'col'), moves))]
    reduce_scatter x0 -> x1, waiting for transfers between devices: none -> 42.9 us  [shards(): part = lax.psum_scatter(total, 'row', scatter_dimension=0, tiled=True)]
    all_to_all x1 -> x0, waiting for transfers between devices: 42.8 us -> none  [shards(): lax.all_to_all(totals, 'col', split_axis=2, concat_axis=2, tiled=True)]
  transfers between devices with their start and end apart: 5 -> 6, of which waited for: 5 -> 5; matrix products, arithmetic and copies ran while one was open for 11% -> 4% of each run, Pallas kernels for 0% -> 0%
where the time goes in v1:
time: 549 us
  waiting for transfers between devices  417 us (76%)
  Pallas kernels  76.3 us (14%)
  other arithmetic  17.6 us (3%)
  between operations  14 us (3%)
  matrix products  11.8 us (2%)
  local copies, waits for them, and re-layouts  8.08 us (1%)
    psum x2, waiting for transfers between devices, spread(): return lax.psum(jnp.where(lax.axis_index(axis) == source, value, 0.0), axis)  202 us
    all_gather x1, waiting for transfers between devices, shards(): lax.all_gather(jnp.concatenate([right, leading[None]], axis=0), 'col', ax...  124 us
    pallas_call x1, Pallas kernels, fused(): pl.pallas_call(functools.partial(fused_kernel, bcols, nb, narrow), grid=(...  76.3 us
    ppermute x2, waiting for transfers between devices, shards(): arrived.append(lax.ppermute(piece, ('row', 'col'), moves))  48.1 us
    reduce_scatter x1, waiting for transfers between devices, shards(): part = lax.psum_scatter(total, 'row', scatter_dimension=0, tiled=True)  42.9 us
    select_n x3, other arithmetic, spread(): return lax.psum(jnp.where(lax.axis_index(axis) == source, value, 0.0), axis)  14.2 us
  transfers between devices with their start and end apart: 6, of which 5 were waited for; matrix products, arithmetic and copies ran while one was open for 4% of the time, Pallas kernels for 0%

profile of v1, /device:TPU:0, one launch (start us, length us, event | category | flops | bytes accessed | tf_op | source)
XLA Modules:
  0.0 548.8 jit_solution(1339125163511019163)
XLA Ops:
  7.2 0.0 all-reduce.6.cloned.1.call-start
  7.2 7.6 %fusion = f32[256,8,256]{2,1,0:T(8,128)S(1)} fusion(pred[]{:T(512)S(6)} %eq.14, f32[16,1,256,8,1,256]{5,4,3,2,1,0:T(1,128)} %param.4), kind=kLoop, calls=%fused_computation.3 | loop fusion | flops 524288 | bytes 4194305 | tf_op jit(solution)/shard_map/jit(_where)/select_n | solution.py:113
  14.8 2.2 copy.23
  17.1 0.6 slice_select_fusion
  17.7 0.0 all-reduce.4.cloned.1.call-start
  17.8 6.0 %broadcast_select_fusion = f32[16,1,256,1,1,256]{5,4,3,2,1,0:T(1,128)S(1)} fusion(pred[]{:T(512)S(6)} %eq.13, f32[16,1,256,8,1,256]{5,4,3,2,1,0:T(1,128)} %param.4), kind=kLoop, calls=%fused_computation | loop fusion | flops 1048576 | bytes 8388609 | tf_op jit(solution)/shard_map/jit(_where)/select_n | solution.py:113
  23.7 2.4 copy.22
  26.2 0.0 all-gather.3.cloned.1.call-start
  26.3 46.8 %all-reduce.6.cloned.1.call-done = (f32[256,2048]{1,0:T(8,128)}, f32[1,64,256]{2,1,0:T(8,128)}) async-done(((f32[256,2048]{1,0:T(8,128)}, f32[1,64,256]{2,1,0:T(8,128)}), (f32[256,2048]{1,0:T(8,128)}, f32[1,64,256]{2,1,0:T(8,128)})) %all-reduce.6.cloned.1.call-update) | async-done | bytes 2162704 | tf_op jit(solution)/shard_map/psum | solution.py:113
  73.1 2.0 pad_maximum_fusion
  75.1 0.2 reduce-scatter.2.cloned.1.call-start
  75.3 3.6 convolution_bitcast_fusion.across_ref
  78.9 154.9 %all-reduce.4.cloned.1.call-done = f32[4096,256]{1,0:T(8,128)} async-done(((f32[4096,256]{1,0:T(8,128)}), f32[4096,256]{1,0:T(8,128)}) %all-reduce.4.cloned.1.call-update) | async-done | bytes 4194320 | tf_op jit(solution)/shard_map/psum | solution.py:113
  233.8 7.6 %fusion.3.panel_ref = f32[4096,256]{1,0:T(8,128)} fusion(f32[4096,256]{1,0:T(8,128)} %all-reduce.4.cloned.1.call-done, f32[256,256]{1,0:T(8,128)S(1)} %copy-done), kind=kOutput, calls=%fused_computation.17 | convolution fusion | flops 3221225472 | bytes 8650752 | tf_op jit(solution)/shard_map/dot_general | solution.py:131
  241.4 124.5 %all-gather.3.cloned.1.call-done = f32[136,64,256]{2,1,0:T(8,128)} async-done(((f32[17,64,256]{2,1,0:T(8,128)}), f32[136,64,256]{2,1,0:T(8,128)}) %all-gather.3.cloned.1.call-update) | async-done | bytes 8912912 | tf_op jit(solution)/shard_map/all_gather | solution.py:129
  365.9 1.1 slice.17
  367.0 0.6 fusion.4.first_ref
  367.6 76.3 %shard_map.67 = (f32[65536,128]{1,0:T(8,128)}, f32[16,64,256]{2,1,0:T(8,128)}, f32[512,2048]{1,0:T(8,128)}) custom-call(f32[65536,128]{1,0:T(8,128)} %bitcast.49, f32[4096,256]{1,0:T(8,128)} %fusion.3.panel_ref, f32[256,2048]{1,0:T(8,128)S(1)} %convolution_bitcast_fusion.across_ref, f32[8,17,64,256]{3,2,1,0:T(8,128)} %bitcast.52, f32[512,256]{1,0:T(8,128)S(1)} %fusion.4.first_ref), custom_call_target="tpu_custom_call" | custom-call | tf_op jit(solution)/shard_map/pallas_call | solution.py:81
  444.0 42.9 %reduce-scatter.2.cloned.1.call-done = f32[128,2048]{1,0:T(8,128)} async-done(((f32[512,2048]{1,0:T(8,128)}), f32[128,2048]{1,0:T(8,128)}) %reduce-scatter.2.cloned.1.call-update) | async-done | bytes 1048592 | tf_op jit(solution)/shard_map/reduce_scatter | solution.py:141
  486.9 1.3 dynamic-slice_bitcast_fusion
  488.2 0.7 collective-permute-start
  488.9 2.7 collective-permute-start.1
  491.6 0.1 broadcast_bitcast_fusion
  491.7 0.1 dynamic_slice.20
  491.8 48.1 %collective-permute-done.1 = f32[64,2048]{1,0:T(8,128)S(1)} collective-permute-done((f32[64,2048]{1,0:T(8,128)S(1)}, f32[64,2048]{1,0:T(8,128)S(1)}, u32[]{:S(2)}, u32[]{:S(2)}) %collective-permute-start.1) | collective-permute-done | bytes 524320 | tf_op jit(solution)/shard_map/ppermute | solution.py:152
  539.8 0.2 fusion.2
  540.0 0.2 copy.25
  540.2 0.2 copy.24
  540.4 0.1 maximum_bitcast_fusion
  540.5 0.3 copy.17
  540.8 0.2 copy-done.3
  541.1 1.2 bitcast_add_fusion
  (14 shorter events, 0.1 us)
Async XLA Ops:
  7.2 68.1 %copy-start = (f32[256,256]{1,0:T(8,128)S(1)}, f32[256,256]{1,0:T(8,128)}, u32[]{:S(2)}) copy-start(f32[256,256]{1,0:T(8,128)} %param.5) | copy-start | bytes 786436
  7.2 65.9 %all-reduce.6.cloned.1.call-start = ((), (), s32[]{:S(2)}) async-start(), calls=%async_computation.4 | async-start | bytes 4325376 | tf_op jit(solution)/shard_map/psum | solution.py:113
  7.2 9.8 %copy-start.2 = (f32[16,1,256,64]{2,3,1,0:T(8,128)S(1)}, f32[16,1,256,64]{2,3,1,0:T(8,128)}, u32[]{:S(2)}) copy-start(f32[16,1,256,64]{2,3,1,0:T(8,128)} %param.6) | copy-start | bytes 3145732
  17.7 216.1 %all-reduce.4.cloned.1.call-start = ((), (), s32[]{:S(2)}) async-start(), calls=%async_computation.1 | async-start | bytes 8388608 | tf_op jit(solution)/shard_map/psum | solution.py:113
  26.2 339.7 %all-gather.3.cloned.1.call-start = ((), (), s32[]{:S(2)}) async-start(), calls=%async_computation.3 | async-start | bytes 10027008 | tf_op jit(solution)/shard_map/all_gather | solution.py:129
  75.1 411.8 %reduce-scatter.2.cloned.1.call-start = ((), (), s32[]{:S(2)}) async-start(), calls=%async_computation.2 | async-start | bytes 5242880 | tf_op jit(solution)/shard_map/reduce_scatter | solution.py:141
  443.9 47.7 %copy-start.4 = (f32[4]{0:T(128)S(1)}, f32[4]{0:T(128)}, u32[]{:S(2)}) copy-start(f32[4]{0:T(128)} %param.7) | copy-start | bytes 52
  488.2 3.6 collective-permute-start
  488.9 51.0 %collective-permute-start.1 = (f32[64,2048]{1,0:T(8,128)S(1)}, f32[64,2048]{1,0:T(8,128)S(1)}, u32[]{:S(2)}, u32[]{:S(2)}) collective-permute-start(f32[64,2048]{1,0:T(8,128)S(1)} %get-tuple-element.22), channel_id=1, source_target_pairs={{0,1},{1,9},{2,17},{3,25},{4,0},{5,8},{6,16},{7,24},{8,3},{9,11},{... | collective-permute-start | bytes 1572872 | tf_op jit(solution)/shard_map/ppermute | solution.py:152
  539.8 1.2 copy-start.3
  540.2 2.1 copy-start.1
Sparse Core Ops, SparseCore 0:
  17.8 55.1 all-reduce.5
  77.3 156.4 all-reduce.3
  236.0 129.8 all-gather.2
  444.1 42.7 reduce-scatter.1

commit v2 on v1

--- a/solution.py
+++ b/solution.py
@@ -109,8 +109,161 @@
     )(tile, panel, across, gathered, first)
 
 
-def spread(value, axis, source):
-    return lax.psum(jnp.where(lax.axis_index(axis) == source, value, 0.0), axis)
+def spread_kernel(ncol, nrow, chunks, column_in, block_in, lead_in,
+                  column_out, block_out, lead_out,
+                  column_send, column_recv, block_send, block_recv,
+                  lead_send, lead_recv, peer_send, peer_recv, local):
+    p = lax.axis_index("row")
+    q = lax.axis_index("col")
+    barrier = pltpu.get_barrier_semaphore()
+    for d in range(1, ncol):
+        pl.semaphore_signal(barrier, inc=1, device_id={"col": (q + d) % ncol})
+    for d in range(1, nrow):
+        pl.semaphore_signal(barrier, inc=1, device_id={"row": (p + d) % nrow})
+    pl.semaphore_wait(barrier, ncol + nrow - 2)
+
+    targets = [(p + 1, jnp.logical_and(p % 2 == 0, p + 1 < nrow)),
+               (p + 2, jnp.logical_and(p % 2 == 0, p + 2 < nrow))]
+
+    def lead_copy(source, way):
+        return pltpu.make_async_remote_copy(
+            source, lead_out.at[q], lead_send.at[way], lead_recv,
+            device_id={"row": targets[way][0] % nrow})
+
+    def peer_copy(source, d):
+        return pltpu.make_async_remote_copy(
+            source, lead_out.at[q], peer_send.at[d], peer_recv.at[d],
+            device_id={"col": (q + d) % ncol})
+
+    def lead_onward(source):
+        for way in range(2):
+            @pl.when(targets[way][1])
+            def _(way=way):
+                lead_copy(source, way).start()
+        for d in range(1, ncol):
+            peer_copy(source, d).start()
+
+    @pl.when(p == 0)
+    def _():
+        pltpu.make_async_copy(lead_in, lead_out.at[q], local).start()
+        lead_onward(lead_in)
+        pltpu.make_async_copy(lead_in, lead_out.at[q], local).wait()
+
+    @pl.when(p > 0)
+    def _():
+        lead_copy(lead_in, 0).wait_recv()
+        lead_onward(lead_out.at[q])
+
+    odd = q % 2
+    place = (1 - odd) * (q // 2) + odd * (ncol - 1 - q // 2)
+
+    def at_place(k):
+        k = k % ncol
+        late = k // (ncol // 2)
+        return (1 - late) * 2 * k + late * (2 * (ncol - 1 - k) + 1)
+
+    ways = [(place, at_place(place + 1)), ((ncol - place) % ncol, at_place(place + ncol - 1))]
+    size = column_in.shape[0] // (2 * chunks)
+    thin = block_in.shape[0] // chunks
+
+    def column_copy(source, way, c):
+        rows = pl.ds(pl.multiple_of((way * chunks + c) * size, size), size)
+        return pltpu.make_async_remote_copy(
+            source.at[rows], column_out.at[rows], column_send.at[way, c],
+            column_recv.at[way, c], device_id={"col": ways[way][1]})
+
+    def block_copy(source, way, c):
+        rows = pl.ds(pl.multiple_of(c * thin, thin), thin)
+        return pltpu.make_async_remote_copy(
+            source.at[rows], block_out.at[rows], block_send.at[way, c],
+            block_recv.at[c], device_id={"row": targets[way][0] % nrow})
+
+    def block_onward(source, c):
+        for way in range(2):
+            @pl.when(targets[way][1])
+            def _(way=way):
+                block_copy(source, way, c).start()
+
+    deep = p // 2 + p % 2
+
+    @pl.loop(0, chunks + ncol + nrow)
+    def _(step):
+        for way in range(2):
+            depth = ways[way][0]
+            c = step - depth
+
+            @pl.when(jnp.logical_and(c >= 0, c < chunks))
+            def _(way=way, depth=depth, c=c):
+                @pl.when(depth == 0)
+                def _():
+                    column_copy(column_in, way, c).start()
+
+                @pl.when(depth > 0)
+                def _():
+                    column_copy(column_in, way, c).wait_recv()
+
+                    @pl.when(depth < ncol - 1)
+                    def _():
+                        column_copy(column_out, way, c).start()
+
+        c = step - deep
+
+        @pl.when(jnp.logical_and(c >= 0, c < chunks))
+        def _():
+            @pl.when(p == 0)
+            def _():
+                block_onward(block_in, c)
+
+            @pl.when(p > 0)
+            def _():
+                block_copy(block_in, 0, c).wait_recv()
+                block_onward(block_out, c)
+
+    @pl.loop(0, chunks)
+    def _(c):
+        for way in range(2):
+            @pl.when(ways[way][0] < ncol - 1)
+            def _(way=way):
+                column_copy(column_in, way, c).wait_send()
+
+            @pl.when(targets[way][1])
+            def _(way=way):
+                block_copy(block_in, way, c).wait_send()
+
+    for way in range(2):
+        @pl.when(targets[way][1])
+        def _(way=way):
+            lead_copy(lead_in, way).wait_send()
+    for d in range(1, ncol):
+        peer_copy(lead_in, d).wait_send()
+        peer_copy(lead_in, d).wait_recv()
+
+
+CHUNKS = 8
+
+
+def spread(column, block, lead, ncol, nrow):
+    dma = pltpu.SemaphoreType.DMA
+    anywhere = pl.BlockSpec(memory_space=pl.ANY)
+    sent = 4 * 2 * (column.size + block.size)
+    return pl.pallas_call(
+        functools.partial(spread_kernel, ncol, nrow, CHUNKS),
+        in_specs=[anywhere] * 3,
+        out_specs=[anywhere] * 3,
+        out_shape=[
+            jax.ShapeDtypeStruct(column.shape, F32),
+            jax.ShapeDtypeStruct(block.shape, F32),
+            jax.ShapeDtypeStruct((ncol,) + lead.shape, F32),
+        ],
+        scratch_shapes=[
+            dma((2, CHUNKS)), dma((2, CHUNKS)), dma((2, CHUNKS)), dma((CHUNKS,)),
+            dma((2,)), dma, dma((ncol,)), dma((ncol,)), dma,
+        ],
+        cost_estimate=pl.CostEstimate(flops=0, bytes_accessed=20 * sent, transcendentals=0),
+        compiler_params=pltpu.CompilerParams(
+            collective_id=0, has_side_effects=True, vmem_limit_bytes=8 * 2**20
+        ),
+    )(column, block, lead)
 
 
 def shards(normal, panel_inverse, rhs, shifts):
@@ -124,14 +277,16 @@
     narrow = rhs.shape[3]
     wide = narrow * ncol
     right = jnp.transpose(rhs[:, 0], (0, 2, 1))
-    across = spread(normal[0, 0].reshape(nb, bcols * nb), "row", 0)
-    leading = spread(right[0], "row", 0)
-    gathered = lax.all_gather(jnp.concatenate([right, leading[None]], axis=0), "col", axis=0)
-    column = spread(normal[:, 0, :, 0, 0, :].reshape(brows * nb, nb), "col", 0)
+    gathered = lax.all_gather(right, "col", axis=0)
+    column_in = normal[:, 0, :, 0, 0, :].reshape(brows * nb, nb)
+    block_in = normal[0, 0].reshape(nb, bcols * nb)
+    column, across, leading = spread(column_in, block_in, right[0], ncol, nrow)
+    column = jnp.where(col_index == 0, column_in, column)
+    across = jnp.where(row_index == 0, block_in, across)
     panel = jnp.dot(column, panel_inverse.T, precision=high, preferred_element_type=F32)
     across = jnp.dot(panel_inverse, across, precision=high, preferred_element_type=F32)
     first = jnp.dot(
-        gathered[:, brows].reshape(wide, nb), panel_inverse.T, precision=high,
+        leading.reshape(wide, nb), panel_inverse.T, precision=high,
         preferred_element_type=F32,
     )
     tile = normal.reshape(brows * nb * bcols * nb // LANES, LANES)

time: 549 us -> 410 us (0.75)
  waiting for transfers between devices: 417 us -> 175 us
  Pallas kernels: 76.3 us -> 185 us
  other arithmetic: 17.6 us -> 1.46 us
  local copies, waits for them, and re-layouts: 8.08 us -> 20.9 us
    psum x2 -> x0, waiting for transfers between devices: 202 us -> none  [spread(): return lax.psum(jnp.where(lax.axis_index(axis) == source, value, 0.0), axis)]
    pallas_call x0 -> x1, Pallas kernels: none -> 108 us  [spread(): pl.pallas_call(functools.partial(spread_kernel, ncol, nrow, CHUNKS), in_s...]
    all_gather x1, waiting for transfers between devices: 124 us -> 33.2 us  [shards(): gathered = lax.all_gather(right, 'col', axis=0)]
    reduce_scatter x1, waiting for transfers between devices: 42.9 us -> 93.4 us  [shards(): part = lax.psum_scatter(total, 'row', scatter_dimension=0, tiled=True)]
    select_n x3 -> x0, other arithmetic: 14.2 us -> none  [spread(): return lax.psum(jnp.where(lax.axis_index(axis) == source, value, 0.0), axis)]
    slice x1 -> x2, local copies, waits for them, and re-layouts: 1.08 us -> 12.2 us  [the longest x1 7.17 us: shards(): block_in = normal[0, 0].reshape(nb, bcols * nb)]
  transfers between devices with their start and end apart: 6 -> 4, of which waited for: 5 -> 3; matrix products, arithmetic and copies ran while one was open for 4% -> 6% of each run, Pallas kernels for 0% -> 26%
where the time goes in v2:
time: 410 us; the launch traced here: 409 us
  Pallas kernels  185 us (45%)
  waiting for transfers between devices  175 us (43%)
  local copies, waits for them, and re-layouts  20.9 us (5%)
  between operations  14.2 us (3%)
  matrix products  9.1 us (2%)
    pallas_call x1, Pallas kernels, spread(): pl.pallas_call(functools.partial(spread_kernel, ncol, nrow, CHUNKS), in_s...  108 us
    reduce_scatter x1, waiting for transfers between devices, shards(): part = lax.psum_scatter(total, 'row', scatter_dimension=0, tiled=True)  93.4 us
    pallas_call x1, Pallas kernels, fused(): pl.pallas_call(functools.partial(fused_kernel, bcols, nb, narrow), grid=(...  76.2 us
    ppermute x2, waiting for transfers between devices, shards(): arrived.append(lax.ppermute(piece, ('row', 'col'), moves))  48 us
    all_gather x1, waiting for transfers between devices, shards(): gathered = lax.all_gather(right, 'col', axis=0)  33.2 us
  transfers between devices with their start and end apart: 4, of which 3 were waited for; matrix products, arithmetic and copies ran while one was open for 6% of the time, Pallas kernels for 26%

profile of v2, /device:TPU:0, one launch (start us, length us, event | category | flops | bytes accessed | tf_op | source)
XLA Modules:
  0.0 409.3 jit_solution(10078976582693622377)
XLA Ops:
  7.2 0.0 copy-start
  7.2 0.0 all-gather.3.cloned.1.call-start
  7.2 0.7 all-gather.3.cloned.1.call-update
  7.9 0.0 reduce-scatter.2.cloned.1.call-start
  8.0 5.1 %slice.9 = f32[16,1,256,1,1,256]{5,4,3,2,1,0:T(1,128)S(1)} slice(f32[16,1,256,8,1,256]{5,4,3,2,1,0:T(1,128)} %param.4), slice={[0:16], [0:1], [0:256], [0:1], [0:1], [0:256]} | slice | bytes 8388608 | tf_op jit(solution)/shard_map/slice | solution.py:281
  13.0 2.4 copy.22
  15.5 7.2 %slice_reduce_fusion = f32[256,8,256]{2,1,0:T(8,128)S(1)} fusion(f32[16,1,256,8,1,256]{5,4,3,2,1,0:T(1,128)} %param.4), kind=kLoop, calls=%fused_computation.4 | loop fusion | bytes 4194304 | tf_op jit(solution)/shard_map/slice | solution.py:282
  22.6 0.9 copy.23
  23.5 0.8 slice_bitcast_fusion.lead_in
  24.4 2.2 copy-done.2
  26.6 108.5 %shard_map.67 = (f32[4096,256]{1,0:T(8,128)S(1)}, f32[256,2048]{1,0:T(8,128)S(1)}, f32[8,64,256]{2,1,0:T(8,128)S(1)}) custom-call(f32[4096,256]{1,0:T(8,128)S(1)} %bitcast.49, f32[256,2048]{1,0:T(8,128)S(1)} %bitcast.51, f32[64,256]{1,0:T(8,128)S(1)} %slice_bitcast_fusion.lead_in), custom_call_target="tpu_custom_call" | custom-call | bytes 251658240 | tf_op jit(solution)/shard_map/pallas_call | solution.py:249
  135.0 0.0 copy-start.3
  135.1 0.6 fusion.7.first_ref
  135.7 3.5 convolution_bitcast_fusion.across_ref
  139.1 5.0 %fusion.panel_ref = f32[4096,256]{1,0:T(8,128)} fusion(f32[256,256]{1,0:T(8,128)S(1)} %copy-done, f32[4096,256]{1,0:T(8,128)S(1)} %bitcast.50, f32[4096,256]{1,0:T(8,128)S(1)} %get-tuple-element.9, pred[]{:T(512)S(6)} %eq.12), kind=kOutput, calls=%fused_computation | convolution fusion | flops 3222274048 | bytes 12845057 | tf_op jit(solution)/shard_map/dot_general | solution.py:286
  144.2 33.2 %all-gather.3.cloned.1.call-done = f32[128,64,256]{2,1,0:T(8,128)} async-done(((f32[16,64,256]{2,1,0:T(8,128)}), f32[128,64,256]{2,1,0:T(8,128)}) %all-gather.3.cloned.1.call-update) | async-done | bytes 8388624 | tf_op jit(solution)/shard_map/all_gather | solution.py:280
  177.4 76.2 %shard_map.68 = (f32[65536,128]{1,0:T(8,128)}, f32[16,64,256]{2,1,0:T(8,128)}, f32[512,2048]{1,0:T(8,128)}) custom-call(f32[65536,128]{1,0:T(8,128)} %bitcast.54, f32[4096,256]{1,0:T(8,128)} %fusion.panel_ref, f32[256,2048]{1,0:T(8,128)S(1)} %copy-done.4, f32[8,16,64,256]{3,2,1,0:T(8,128)} %bitcast.56, f32[512,256]{1,0:T(8,128)S(1)} %fusion.7.first_ref), custom_call_target="tpu_custom_call" | custom-call | tf_op jit(solution)/shard_map/pallas_call | solution.py:81
  253.6 0.0 reduce-scatter.2.cloned.1.call-update
  253.7 93.4 %reduce-scatter.2.cloned.1.call-done = f32[128,2048]{1,0:T(8,128)} async-done(((f32[512,2048]{1,0:T(8,128)}), f32[128,2048]{1,0:T(8,128)}) %reduce-scatter.2.cloned.1.call-update) | async-done | bytes 1048592 | tf_op jit(solution)/shard_map/reduce_scatter | solution.py:296
  347.1 1.3 dynamic-slice_bitcast_fusion
  348.4 0.7 collective-permute-start
  349.1 2.8 collective-permute-start.1
  351.9 0.1 broadcast_bitcast_fusion
  351.9 0.1 dynamic_slice.20
  352.0 48.0 %collective-permute-done.1 = f32[64,2048]{1,0:T(8,128)S(1)} collective-permute-done((f32[64,2048]{1,0:T(8,128)S(1)}, f32[64,2048]{1,0:T(8,128)S(1)}, u32[]{:S(2)}, u32[]{:S(2)}) %collective-permute-start.1) | collective-permute-done | bytes 524320 | tf_op jit(solution)/shard_map/ppermute | solution.py:307
  400.0 0.2 fusion.6
  400.2 0.2 copy.25
  400.4 0.2 copy.24
  400.6 0.1 maximum_bitcast_fusion
  400.7 0.3 copy.17
  401.0 0.2 copy-done.5
  401.3 1.2 bitcast_add_fusion
  (11 shorter events, 0.0 us)
Async XLA Ops:
  7.2 127.9 %copy-start = (f32[256,256]{1,0:T(8,128)S(1)}, f32[256,256]{1,0:T(8,128)}, u32[]{:S(2)}) copy-start(f32[256,256]{1,0:T(8,128)} %param.5) | copy-start | bytes 786436
  7.2 170.2 %all-gather.3.cloned.1.call-start = ((), (), s32[]{:S(2)}) async-start(), calls=%async_computation.2 | async-start | bytes 9437184 | tf_op jit(solution)/shard_map/all_gather | solution.py:280
  7.9 339.2 %reduce-scatter.2.cloned.1.call-start = ((), (), s32[]{:S(2)}) async-start(), calls=%async_computation.1 | async-start | bytes 5242880 | tf_op jit(solution)/shard_map/reduce_scatter | solution.py:296
  24.4 2.2 copy-start.2
  135.0 4.1 %copy-start.3 = (f32[16,1,256,1,1,256]{5,2,3,4,1,0:T(8,128)S(1)}, f32[16,1,256,1,1,256]{5,2,3,4,1,0:T(8,128)}, u32[]{:S(2)}) copy-start(f32[16,1,256,1,1,256]{5,2,3,4,1,0:T(8,128)} %copy.22) | copy-start | bytes 12582916
  139.1 38.2 %copy-start.4 = (f32[256,2048]{1,0:T(8,128)S(1)}, f32[256,2048]{1,0:T(8,128)}, u32[]{:S(2)}) copy-start(f32[256,2048]{1,0:T(8,128)} %convolution_bitcast_fusion.across_ref) | copy-start | bytes 6291460
  253.6 98.2 %copy-start.6 = (f32[4]{0:T(128)S(1)}, f32[4]{0:T(128)}, u32[]{:S(2)}) copy-start(f32[4]{0:T(128)} %param.7) | copy-start | bytes 52
  348.4 3.6 collective-permute-start
  349.1 50.9 %collective-permute-start.1 = (f32[64,2048]{1,0:T(8,128)S(1)}, f32[64,2048]{1,0:T(8,128)S(1)}, u32[]{:S(2)}, u32[]{:S(2)}) collective-permute-start(f32[64,2048]{1,0:T(8,128)S(1)} %get-tuple-element.26), channel_id=1, source_target_pairs={{0,1},{1,9},{2,17},{3,25},{4,0},{5,8},{6,16},{7,24},{8,3},{9,11},{... | collective-permute-start | bytes 1572872 | tf_op jit(solution)/shard_map/ppermute | solution.py:307
  400.0 1.2 copy-start.5
  400.4 2.1 copy-start.1
Sparse Core Ops, SparseCore 0:
  10.1 167.2 all-gather.2
  253.8 93.2 reduce-scatter.1

commit v3 on v2

--- a/solution.py
+++ b/solution.py
@@ -34,7 +34,7 @@
 
 
 def fused_kernel(bcols, nb, narrow, tile_ref, panel_ref, across_ref, rhs_ref, first_ref,
-                 schur_ref, own_ref, total_ref, across3, first3, reduced):
+                 schur_ref, own_ref, rest_ref, total_ref, across3, first3, reduced):
     step = pl.program_id(0)
     stride = bcols * nb // LANES
     per = nb // LANES
@@ -59,7 +59,19 @@
     reduced[...] = value
     mine = pl.multiple_of(lax.axis_index("col") * narrow, narrow)
     own_ref[0] = reduced[pl.ds(mine, narrow), :]
-    value3 = left_of(value)
+    nrow = lax.axis_size("row")
+    spacing = lax.axis_size("col") // nrow
+    offset = lax.axis_index("col") // nrow
+    groups = []
+    for t in range(spacing):
+        which = (offset + t) % spacing
+        groups.append(jnp.concatenate([
+            reduced[pl.ds(pl.multiple_of((p * spacing + which) * narrow, narrow), narrow), :]
+            for p in range(nrow)
+        ], axis=0))
+    for t in range(1, spacing):
+        rest_ref[t - 1, 0] = groups[t]
+    value3 = left_of(groups[0])
     for b in range(bcols):
         columns = slice(b * nb, (b + 1) * nb)
         product = dot(panel3, across3[:, columns])
@@ -77,6 +89,9 @@
     wide = first.shape[0]
     ncol = wide // narrow
     chunk = nb * bcols * nb // LANES
+    spacing = ncol // lax.axis_size("row")
+    group = wide // spacing
+    rest = max(spacing - 1, 1)
     whole = lambda i: (0, 0)
     return pl.pallas_call(
         functools.partial(fused_kernel, bcols, nb, narrow),
@@ -91,12 +106,14 @@
         out_specs=[
             pl.BlockSpec((chunk, LANES), lambda i: (i, 0)),
             pl.BlockSpec((1, narrow, nb), lambda i: (i, 0, 0)),
-            pl.BlockSpec((wide, bcols * nb), whole),
+            pl.BlockSpec((rest, 1, group, nb), lambda i: (0, i, 0, 0)),
+            pl.BlockSpec((group, bcols * nb), whole),
         ],
         out_shape=[
             jax.ShapeDtypeStruct(tile.shape, F32),
             jax.ShapeDtypeStruct((brows, narrow, nb), F32),
-            jax.ShapeDtypeStruct((wide, bcols * nb), F32),
+            jax.ShapeDtypeStruct((rest, brows, group, nb), F32),
+            jax.ShapeDtypeStruct((group, bcols * nb), F32),
         ],
         scratch_shapes=[
             pltpu.VMEM((3 * nb, bcols * nb), BF16),
@@ -107,6 +124,44 @@
             dimension_semantics=("arbitrary",), vmem_limit_bytes=48 * 2**20
         ),
     )(tile, panel, across, gathered, first)
+
+
+def later_kernel(bcols, nb, schur_ref, value_ref, total_ref):
+    stride = bcols * nb // LANES
+    per = nb // LANES
+
+    @pl.when(pl.program_id(0) == 0)
+    def _():
+        total_ref[...] = jnp.zeros_like(total_ref)
+
+    value3 = left_of(value_ref[...])
+    for b in range(bcols):
+        updated = jnp.concatenate([
+            schur_ref[pl.ds(b * per + h, nb, stride=stride), :] for h in range(per)
+        ], axis=1)
+        total_ref[:, b * nb:(b + 1) * nb] += dot(value3, right_of(updated))
+
+
+def later(schur, values, index, bcols, nb):
+    brows, group = values.shape[1:3]
+    chunk = nb * bcols * nb // LANES
+    return pl.pallas_call(
+        functools.partial(later_kernel, bcols, nb),
+        grid=(brows,),
+        in_specs=[
+            pl.BlockSpec((chunk, LANES), lambda i: (i, 0)),
+            pl.BlockSpec((None, None, group, nb), lambda i: (index, i, 0, 0)),
+        ],
+        out_specs=pl.BlockSpec((group, bcols * nb), lambda i: (0, 0)),
+        out_shape=jax.ShapeDtypeStruct((group, bcols * nb), F32),
+        cost_estimate=pl.CostEstimate(
+            flops=6 * schur.size * group, bytes_accessed=4 * (schur.size + brows * group * nb),
+            transcendentals=0,
+        ),
+        compiler_params=pltpu.CompilerParams(
+            dimension_semantics=("arbitrary",), vmem_limit_bytes=32 * 2**20
+        ),
+    )(schur, values)
 
 
 def spread_kernel(ncol, nrow, chunks, column_in, block_in, lead_in,
@@ -290,12 +345,9 @@
         preferred_element_type=F32,
     )
     tile = normal.reshape(brows * nb * bcols * nb // LANES, LANES)
-    schur, reduced, total = fused(
+    schur, reduced, values, total = fused(
         tile, panel, across, gathered, first, brows, bcols, nb, narrow
     )
-    part = lax.psum_scatter(total, "row", scatter_dimension=0, tiled=True)
-    part = part.reshape(spacing, narrow, bcols * nb)
-    offset = col_index // nrow
     arrived = []
     for t in range(spacing):
         moves = [
@@ -303,7 +355,9 @@
             for p in range(nrow)
             for q in range(ncol)
         ]
-        piece = lax.dynamic_index_in_dim(part, (offset + t) % spacing, 0, keepdims=False)
+        if t > 0:
+            total = later(schur, values, t - 1, bcols, nb)
+        piece = lax.psum_scatter(total, "row", scatter_dimension=0, tiled=True)
         arrived.append(lax.ppermute(piece, ("row", "col"), moves))
     arrived = jnp.stack(arrived)
     place = col_index % spacing

time: 410 us -> 387 us (0.944)
  waiting for transfers between devices: 175 us -> 141 us
  Pallas kernels: 185 us -> 194 us
    pallas_call x0 -> x1, Pallas kernels: none -> 27.8 us  [later(): pl.pallas_call(functools.partial(later_kernel, bcols, nb), grid=(brows,),...]
    ppermute x2, waiting for transfers between devices: 48 us -> 25 us  [shards(): arrived.append(lax.ppermute(piece, ('row', 'col'), moves))]
    pallas_call x1, Pallas kernels: 76.2 us -> 57.9 us  [fused(): pl.pallas_call(functools.partial(fused_kernel, bcols, nb, narrow), grid=(...]
    reduce_scatter x1 -> x2, waiting for transfers between devices: 93.4 us -> 82.1 us  [shards(): piece = lax.psum_scatter(total, 'row', scatter_dimension=0, tiled=True)]
    unnamed x18 -> x22, local copies, waits for them, and re-layouts: 6.11 us -> 9.63 us
  transfers between devices with their start and end apart: 4 -> 5, of which waited for: 3 -> 4; matrix products, arithmetic and copies ran while one was open for 6% -> 7% of each run, Pallas kernels for 26% -> 35%
where the time goes in v3:
time: 387 us; the launch traced here: 386 us
  Pallas kernels  194 us (50%)
  waiting for transfers between devices  141 us (36%)
  local copies, waits for them, and re-layouts  23.2 us (6%)
  between operations  13.9 us (4%)
  matrix products  9.12 us (2%)
    pallas_call x1, Pallas kernels, spread(): pl.pallas_call(functools.partial(spread_kernel, ncol, nrow, CHUNKS), in_s...  108 us
    reduce_scatter x2, waiting for transfers between devices, shards(): piece = lax.psum_scatter(total, 'row', scatter_dimension=0, tiled=True)  82.1 us
    pallas_call x1, Pallas kernels, fused(): pl.pallas_call(functools.partial(fused_kernel, bcols, nb, narrow), grid=(...  57.9 us
    all_gather x1, waiting for transfers between devices, shards(): gathered = lax.all_gather(right, 'col', axis=0)  33.2 us
    pallas_call x1, Pallas kernels, later(): pl.pallas_call(functools.partial(later_kernel, bcols, nb), grid=(brows,),...  27.8 us
    ppermute x2, waiting for transfers between devices, shards(): arrived.append(lax.ppermute(piece, ('row', 'col'), moves))  25 us
    unnamed x22, local copies, waits for them, and re-layouts  9.63 us
  transfers between devices with their start and end apart: 5, of which 4 were waited for; matrix products, arithmetic and copies ran while one was open for 7% of the time, Pallas kernels for 35%

profile of v3, /device:TPU:0, one launch (start us, length us, event | category | flops | bytes accessed | tf_op | source)
XLA Modules:
  0.0 386.0 jit_solution(5226042722502802474)
XLA Ops:
  7.2 0.7 all-gather.3.cloned.1.call-update
  7.9 0.0 reduce-scatter.3.cloned.1.call-start
  8.0 5.1 %slice.9 = f32[16,1,256,1,1,256]{5,4,3,2,1,0:T(1,128)S(1)} slice(f32[16,1,256,8,1,256]{5,4,3,2,1,0:T(1,128)} %param.4), slice={[0:16], [0:1], [0:256], [0:1], [0:1], [0:256]} | slice | bytes 8388608 | tf_op jit(solution)/shard_map/slice | solution.py:336
  13.0 2.4 copy.22
  15.5 7.2 %slice_reduce_fusion = f32[256,8,256]{2,1,0:T(8,128)S(1)} fusion(f32[16,1,256,8,1,256]{5,4,3,2,1,0:T(1,128)} %param.4), kind=kLoop, calls=%fused_computation.4 | loop fusion | bytes 4194304 | tf_op jit(solution)/shard_map/slice | solution.py:337
  22.6 0.9 copy.23
  23.5 0.8 slice_bitcast_fusion.lead_in
  24.4 2.2 copy-done.2
  26.6 108.5 %shard_map.67 = (f32[4096,256]{1,0:T(8,128)S(1)}, f32[256,2048]{1,0:T(8,128)S(1)}, f32[8,64,256]{2,1,0:T(8,128)S(1)}) custom-call(f32[4096,256]{1,0:T(8,128)S(1)} %bitcast.44, f32[256,2048]{1,0:T(8,128)S(1)} %bitcast.46, f32[64,256]{1,0:T(8,128)S(1)} %slice_bitcast_fusion.lead_in), custom_call_target="tpu_custom_call" | custom-call | bytes 251658240 | tf_op jit(solution)/shard_map/pallas_call | solution.py:304
  135.1 0.6 fusion.7.first_ref
  135.7 3.5 convolution_bitcast_fusion.across_ref
  139.2 5.0 %fusion.panel_ref = f32[4096,256]{1,0:T(8,128)} fusion(f32[256,256]{1,0:T(8,128)S(1)} %copy-done, f32[4096,256]{1,0:T(8,128)S(1)} %bitcast.45, f32[4096,256]{1,0:T(8,128)S(1)} %get-tuple-element.10, pred[]{:T(512)S(6)} %eq.10), kind=kOutput, calls=%fused_computation | convolution fusion | flops 3222274048 | bytes 12845057 | tf_op jit(solution)/shard_map/dot_general | solution.py:341
  144.2 33.2 %all-gather.3.cloned.1.call-done = f32[128,64,256]{2,1,0:T(8,128)} async-done(((f32[16,64,256]{2,1,0:T(8,128)}), f32[128,64,256]{2,1,0:T(8,128)}) %all-gather.3.cloned.1.call-update) | async-done | bytes 8388624 | tf_op jit(solution)/shard_map/all_gather | solution.py:335
  177.4 57.9 %shard_map.68 = (f32[65536,128]{1,0:T(8,128)}, f32[16,64,256]{2,1,0:T(8,128)}, f32[1,16,256,256]{3,2,1,0:T(8,128)}, f32[256,2048]{1,0:T(8,128)S(1)}) custom-call(f32[65536,128]{1,0:T(8,128)} %bitcast.49, f32[4096,256]{1,0:T(8,128)} %fusion.panel_ref, f32[256,2048]{1,0:T(8,128)S(1)} %copy-done.4, f32[8,16,64,256]{3,2,1,0:T(8,128)} %bitcast.51, ...), custom_call_target="tpu_custom_call" | custom-call | tf_op jit(solution)/shard_map/pallas_call | solution.py:96
  235.3 1.3 copy-done.5
  236.7 0.0 reduce-scatter.5.cloned.1.call-start
  236.7 2.2 copy-done.6
  238.9 27.8 %shard_map.69 = f32[256,2048]{1,0:T(8,128)} custom-call(f32[65536,128]{1,0:T(8,128)} %get-tuple-element.13.schur_ref, f32[1,16,256,256]{3,2,1,0:T(8,128)S(1)} %copy-done.6), custom_call_target="tpu_custom_call" | custom-call | flops 12884901888 | bytes 37748736 | tf_op jit(solution)/shard_map/pallas_call | solution.py:148
  266.7 50.1 %reduce-scatter.3.cloned.1.call-done = f32[64,2048]{1,0:T(8,128)} async-done(((f32[256,2048]{1,0:T(8,128)}), f32[64,2048]{1,0:T(8,128)}) %reduce-scatter.3.cloned.1.call-update) | async-done | bytes 524304 | tf_op jit(solution)/shard_map/reduce_scatter | solution.py:360
  316.8 1.7 collective-permute-start
  318.5 32.0 %reduce-scatter.5.cloned.1.call-done = f32[64,2048]{1,0:T(8,128)} async-done(((f32[256,2048]{1,0:T(8,128)}), f32[64,2048]{1,0:T(8,128)}) %reduce-scatter.5.cloned.1.call-update) | async-done | bytes 524304 | tf_op jit(solution)/shard_map/reduce_scatter | solution.py:360
  350.5 1.5 collective-permute-start.1
  352.0 0.1 broadcast_bitcast_fusion
  352.0 0.1 dynamic_slice.12
  352.1 25.0 %collective-permute-done.1 = f32[64,2048]{1,0:T(8,128)S(1)} collective-permute-done((f32[64,2048]{1,0:T(8,128)}, f32[64,2048]{1,0:T(8,128)S(1)}, u32[]{:S(2)}, u32[]{:S(2)}) %collective-permute-start.1) | collective-permute-done | bytes 524320 | tf_op jit(solution)/shard_map/ppermute | solution.py:361
  377.1 0.2 fusion.6
  377.3 0.2 copy.25
  377.5 0.2 copy.24
  377.6 0.1 maximum_bitcast_fusion
  377.7 0.3 copy.17
  378.1 0.2 copy-done.7
  378.3 1.2 bitcast_add_fusion
  (18 shorter events, 0.1 us)
Async XLA Ops:
  7.2 127.9 %copy-start = (f32[256,256]{1,0:T(8,128)S(1)}, f32[256,256]{1,0:T(8,128)}, u32[]{:S(2)}) copy-start(f32[256,256]{1,0:T(8,128)} %param.5) | copy-start | bytes 786436
  7.2 170.2 %all-gather.3.cloned.1.call-start = ((), (), s32[]{:S(2)}) async-start(), calls=%async_computation.4 | async-start | bytes 9437184 | tf_op jit(solution)/shard_map/all_gather | solution.py:335
  7.9 308.9 %reduce-scatter.3.cloned.1.call-start = ((), (), s32[]{:S(2)}) async-start(), calls=%async_computation.2 | async-start | bytes 2621440 | tf_op jit(solution)/shard_map/reduce_scatter | solution.py:360
  24.4 2.2 copy-start.2
  135.0 4.1 %copy-start.3 = (f32[16,1,256,1,1,256]{5,2,3,4,1,0:T(8,128)S(1)}, f32[16,1,256,1,1,256]{5,2,3,4,1,0:T(8,128)}, u32[]{:S(2)}) copy-start(f32[16,1,256,1,1,256]{5,2,3,4,1,0:T(8,128)} %copy.22) | copy-start | bytes 12582916
  139.2 38.2 %copy-start.4 = (f32[256,2048]{1,0:T(8,128)S(1)}, f32[256,2048]{1,0:T(8,128)}, u32[]{:S(2)}) copy-start(f32[256,2048]{1,0:T(8,128)} %convolution_bitcast_fusion.across_ref) | copy-start | bytes 6291460
  235.3 1.3 copy-start.5
  236.7 113.8 %reduce-scatter.5.cloned.1.call-start = ((), (), s32[]{:S(2)}) async-start(), calls=%async_computation.3 | async-start | bytes 2621440 | tf_op jit(solution)/shard_map/reduce_scatter | solution.py:360
  236.7 2.2 copy-start.6
  238.9 113.0 %copy-start.8 = (f32[4]{0:T(128)S(1)}, f32[4]{0:T(128)}, u32[]{:S(2)}) copy-start(f32[4]{0:T(128)} %param.7) | copy-start | bytes 52
  316.8 35.3 %collective-permute-start = (f32[64,2048]{1,0:T(8,128)}, f32[64,2048]{1,0:T(8,128)S(1)}, u32[]{:S(2)}, u32[]{:S(2)}) collective-permute-start(f32[64,2048]{1,0:T(8,128)} %reduce-scatter.3.cloned.1.call-done), channel_id=1, source_target_pairs={{0,0},{1,8},{2,16},{3,24},{4,1},{5,9},{6,17},{7,25},{8,2},{9,10},{... | collective-permute-start | bytes 1572872 | tf_op jit(solution)/shard_map/ppermute | solution.py:361
  350.5 26.6 %collective-permute-start.1 = (f32[64,2048]{1,0:T(8,128)}, f32[64,2048]{1,0:T(8,128)S(1)}, u32[]{:S(2)}, u32[]{:S(2)}) collective-permute-start(f32[64,2048]{1,0:T(8,128)} %reduce-scatter.5.cloned.1.call-done), channel_id=1, source_target_pairs={{0,1},{1,9},{2,17},{3,25},{4,0},{5,8},{6,16},{7,24},{8,3},{9,11},{... | collective-permute-start | bytes 1572872 | tf_op jit(solution)/shard_map/ppermute | solution.py:361
  377.1 1.2 copy-start.7
  377.5 2.0 copy-start.1
Sparse Core Ops, SparseCore 0:
  10.1 167.2 all-gather.2
  236.8 79.9 reduce-scatter.2
  319.3 31.1 reduce-scatter.4
